TPU v7x, 32 devices: a whole 2x2x4 slice. The times are simulated.
32 devices in a mesh: tensor: 4 (over z), dp: 2 (over y), section: 4 (over x, core).
Axes of the slice: x: 2, y: 2, z: 4, core: 2. Of those that a mesh axis runs over, the one named last changes fastest.
Arguments:
- basis_grad: bfloat16 [14336, 14336], P(('dp', 'section'), 'tensor'), may hold values from -0.046875 to 0.046875
- query: bfloat16 [14336, 4096], P('tensor', ('dp', 'section')), may hold values from -6 to 6
- basis_act: bfloat16 [4096, 4096], P(('dp', 'section'), 'tensor'), may hold values from -0.09375 to 0.09375
- eig_vals: float32 [14336, 4096], P(('dp', 'section'), 'tensor'), may hold values from 0.05 to 5
- grad_out: bfloat16 [512, 14336], P('section', 'tensor'), may hold values from -0.046875 to 0.046875
- act_in: bfloat16 [512, 4096], P('section', 'tensor'), may hold values from -0.09375 to 0.09375
Outputs:
- precond: bfloat16 [14336, 4096], P(('dp', 'section'), 'tensor')
- scores: float32 [512], P('tensor')
All inputs are finite; a program needn't handle non-finite values.
Results may differ from a plain program's by a relative error of at most 0.015.
Values may be sent and summed in bfloat16 or wider, within the bound.
No kernel may reach another device: no remote copies, remote signals or barrier semaphores. Data moves between devices by JAX's collectives and lax.ppermute only.
A program may use at most 128 MiB of HBM per device.

v0:
```python
import jax
import jax.numpy as jnp
from jax import lax
from jax.sharding import PartitionSpec as P

damping = 0.1


def body(basis_grad, query, basis_act, eig_vals, grad_out, act_in):
    partial_rows = jnp.dot(
        basis_grad,
        lax.all_gather(query, ("dp", "section"), axis=1, tiled=True),
        preferred_element_type=jnp.float32,
    )
    basis_cols = lax.all_gather(basis_act, ("dp", "section"), axis=0, tiled=True)
    summed_rows = lax.psum(partial_rows.astype(jnp.bfloat16), "tensor")
    rotated = jnp.dot(summed_rows, basis_cols, preferred_element_type=jnp.float32)
    precond = (rotated / (eig_vals + damping)).astype(jnp.bfloat16)
    grad_all = lax.all_gather(grad_out, "section", axis=0, tiled=True)
    grad_rot = jnp.einsum("ei,ti->et", basis_grad, grad_all, preferred_element_type=jnp.float32)
    act_rows = lax.all_gather(act_in, "tensor", axis=1, tiled=True)
    act_rot = jnp.dot(act_rows, basis_cols, preferred_element_type=jnp.float32).astype(jnp.bfloat16)
    act_all = lax.all_gather(act_rot, "section", axis=0, tiled=True)
    weighted = jnp.einsum("ek,tk->et", precond, act_all, preferred_element_type=jnp.float32)
    grad_share, weighted_share = (
        lax.psum_scatter(grad_rot, "tensor", scatter_dimension=1, tiled=True),
        lax.psum_scatter(weighted, "tensor", scatter_dimension=1, tiled=True),
    )
    partial_value = jnp.sum(grad_share * weighted_share, axis=0)
    scores = lax.psum(partial_value, ("dp", "section"))
    return (precond, scores)


def solution(mesh):
    return jax.shard_map(
        body,
        mesh=mesh,
        in_specs=(
            P(("dp", "section"), "tensor"),
            P("tensor", ("dp", "section")),
            P(("dp", "section"), "tensor"),
            P(("dp", "section"), "tensor"),
            P("section", "tensor"),
            P("section", "tensor"),
        ),
        out_specs=(P(("dp", "section"), "tensor"), P("tensor")),
        check_vma=False,
    )
```

profile of v0, /device:TPU:0, one launch (start us, length us, event | category | flops | bytes accessed | tf_op | source)
XLA Modules:
  0.0 956.8 jit_solution(12993212989069728752)
XLA Ops:
  7.2 0.0 all-gather.6.cloned.1.call-start
  7.2 0.7 all-gather.6.cloned.1.call-update
  7.9 0.0 all-gather.12.cloned.1.call-start
  7.9 0.7 all-gather.12.cloned.1.call-update
  8.6 0.0 all-gather.8.cloned.1.call-start
  8.7 0.7 all-gather.8.cloned.1.call-update
  9.4 0.0 all-gather.10.cloned.1.call-start
  9.4 0.5 all-gather.10.cloned.1.call-update
  10.0 0.0 all-reduce.2.cloned.1.call-start
  10.0 151.4 %all-gather.6.cloned.1.call-done = bf16[3584,4096]{1,0:T(8,128)(2,1)} async-done(((bf16[3584,512]{1,0:T(8,128)(2,1)}), bf16[3584,4096]{1,0:T(8,128)(2,1)}) %all-gather.6.cloned.1.call-update) | async-done | bytes 29360144 | tf_op jit(solution)/shard_map/all_gather | solution.py:12
  161.4 61.9 %convolution_convert_fusion = bf16[1792,4096]{1,0:T(8,128)(2,1)} fusion(bf16[1792,3584]{1,0:T(8,128)(2,1)} %param.6, bf16[3584,4096]{1,0:T(8,128)(2,1)} %all-gather.6.cloned.1.call-done), kind=kOutput, calls=%fused_computation | convolution fusion | flops 52620689408 | bytes 56885248 | tf_op jit(solution)/shard_map/dot_general | solution.py:10
  223.3 0.0 all-reduce.2.cloned.1.call-update
  223.3 0.0 all-gather.14.cloned.1.call-start
  223.4 0.0 all-gather.12.cloned.1.call-done
  223.4 23.1 %all-gather.8.cloned.1.call-done = bf16[4096,1024]{1,0:T(8,128)(2,1)} async-done(((bf16[512,1024]{1,0:T(8,128)(2,1)}), bf16[4096,1024]{1,0:T(8,128)(2,1)}) %all-gather.8.cloned.1.call-update) | async-done | bytes 8388624 | tf_op jit(solution)/shard_map/all_gather | solution.py:15
  246.5 5.7 convolution_convert_fusion.1
  252.2 0.0 all-gather.14.cloned.1.call-update
  252.2 0.0 reduce-scatter.3.cloned.1.call-start
  252.3 27.2 %all-gather.10.cloned.1.call-done = bf16[512,3584]{1,0:T(8,128)(2,1)} async-done(((bf16[128,3584]{1,0:T(8,128)(2,1)}), bf16[512,3584]{1,0:T(8,128)(2,1)}) %all-gather.10.cloned.1.call-update) | async-done | bytes 3670032 | tf_op jit(solution)/shard_map/all_gather | solution.py:19
  279.4 12.1 %fusion = f32[1792,512]{1,0:T(8,128)} fusion(bf16[1792,3584]{1,0:T(8,128)(2,1)} %param.6, bf16[512,3584]{1,0:T(8,128)(2,1)} %all-gather.10.cloned.1.call-done), kind=kOutput, calls=%fused_computation.4 | convolution fusion | flops 6576668672 | bytes 20185088 | tf_op jit(solution)/shard_map/ei,ti->et/dot_general | solution.py:20
  291.6 0.0 reduce-scatter.3.cloned.1.call-update
  291.6 0.2 reduce-scatter.5.cloned.1.call-start
  291.8 483.7 %all-reduce.2.cloned.1.call-done = bf16[1792,4096]{1,0:T(8,128)(2,1)} async-done(((bf16[1792,4096]{1,0:T(8,128)(2,1)}), bf16[1792,4096]{1,0:T(8,128)(2,1)}) %all-reduce.2.cloned.1.call-update) | async-done | bytes 14680080 | tf_op jit(solution)/shard_map/psum | solution.py:16
  775.5 22.4 %divide_convert_fusion = bf16[1792,1024]{1,0:T(8,128)(2,1)} fusion(f32[1792,1024]{1,0:T(8,128)} %param.9, bf16[1792,4096]{1,0:T(8,128)(2,1)} %all-reduce.2.cloned.1.call-done, bf16[4096,1024]{1,0:T(8,128)(2,1)} %all-gather.8.cloned.1.call-done), kind=kOutput, calls=%fused_computation.1 | convolution fusion | flops 15037890560 | bytes 34078720 | tf_op jit(solution)/shard_map/dot_general | solution.py:17
  797.9 0.0 all-gather.14.cloned.1.call-done
  798.0 6.2 fusion.1
  804.2 0.0 reduce-scatter.5.cloned.1.call-update
  804.2 59.2 %reduce-scatter.3.cloned.1.call-done = f32[1792,128]{1,0:T(8,128)} async-done(((f32[1792,512]{1,0:T(8,128)}), f32[1792,128]{1,0:T(8,128)}) %reduce-scatter.3.cloned.1.call-update) | async-done | bytes 917520 | tf_op jit(solution)/shard_map/reduce_scatter | solution.py:26
  863.4 71.2 %reduce-scatter.5.cloned.1.call-done = f32[1792,128]{1,0:T(8,128)} async-done(((f32[1792,512]{1,0:T(8,128)}), f32[1792,128]{1,0:T(8,128)}) %reduce-scatter.5.cloned.1.call-update) | async-done | bytes 917520 | tf_op jit(solution)/shard_map/reduce_scatter | solution.py:27
  934.6 1.7 multiply_reduce_fusion
  936.3 13.7 %psum.15 = f32[128]{0:T(128)} all-reduce(f32[128]{0:T(128)S(1)} %multiply_reduce_fusion), channel_id=1, replica_groups=mesh['tensor'=4,'dp'=2,'section'=4] {'dp','section'}, use_global_device_ids=true, to_apply=%region_4.0 | all-reduce | flops 128 | bytes 1024 | tf_op jit(solution)/shard_map/psum | solution.py:30
Async XLA Ops:
  7.2 154.2 %all-gather.6.cloned.1.call-start = ((), (), s32[]{:S(2)}) async-start(), calls=%async_computation.2 | async-start | bytes 33030144 | tf_op jit(solution)/shard_map/all_gather | solution.py:12
  7.9 215.5 %all-gather.12.cloned.1.call-start = ((), (), s32[]{:S(2)}) async-start(), calls=%async_computation.7 | async-start | bytes 1310720 | tf_op jit(solution)/shard_map/all_gather | solution.py:21
  8.6 237.9 %all-gather.8.cloned.1.call-start = ((), (), s32[]{:S(2)}) async-start(), calls=%async_computation.4 | async-start | bytes 9437184 | tf_op jit(solution)/shard_map/all_gather | solution.py:15
  9.4 270.0 %all-gather.10.cloned.1.call-start = ((), (), s32[]{:S(2)}) async-start(), calls=%async_computation.5 | async-start | bytes 4587520 | tf_op jit(solution)/shard_map/all_gather | solution.py:19
  10.0 765.6 %all-reduce.2.cloned.1.call-start = ((), (), s32[]{:S(2)}) async-start(), calls=%async_computation.3 | async-start | bytes 29360128 | tf_op jit(solution)/shard_map/psum | solution.py:16
  223.3 574.6 %all-gather.14.cloned.1.call-start = ((), (), s32[]{:S(2)}) async-start(), calls=%async_computation.8 | async-start | bytes 1310720 | tf_op jit(solution)/shard_map/all_gather | solution.py:23
  252.2 611.2 %reduce-scatter.3.cloned.1.call-start = ((), (), s32[]{:S(2)}) async-start(), calls=%async_computation.6 | async-start | bytes 4587520 | tf_op jit(solution)/shard_map/reduce_scatter | solution.py:26
  291.6 643.0 %reduce-scatter.5.cloned.1.call-start = ((), (), s32[]{:S(2)}) async-start(), calls=%async_computation.9 | async-start | bytes 4587520 | tf_op jit(solution)/shard_map/reduce_scatter | solution.py:27
Sparse Core Ops, SparseCore 0:
  9.8 151.4 all-gather.5
  162.9 27.9 all-gather.11
  192.8 53.6 all-gather.7
  247.9 31.4 all-gather.9
  281.8 493.7 all-reduce.1
  776.9 15.5 all-gather.13
  794.8 68.5 reduce-scatter.2
  865.7 68.8 reduce-scatter.4
where the time goes:
time: 957 us
  waiting for transfers between devices  818 us (85%)
  matrix products  108 us (11%)
  between operations  14.1 us (1%)
  blocking collectives  13.7 us (1%)
    psum x1, waiting for transfers between devices, body(): summed_rows = lax.psum(partial_rows.astype(jnp.bfloat16), 'tensor')  484 us
    all_gather x1, waiting for transfers between devices, body(): lax.all_gather(query, ('dp', 'section'), axis=1, tiled=True)  151 us
    reduce_scatter x1, waiting for transfers between devices, body(): lax.psum_scatter(weighted, 'tensor', scatter_dimension=1, tiled=True)  71.2 us
    dot_general x1, matrix products, body(): jnp.dot(basis_grad, lax.all_gather(query, ('dp', 'section'), axis=1, tile...  61.9 us
    reduce_scatter x1, waiting for transfers between devices, body(): lax.psum_scatter(grad_rot, 'tensor', scatter_dimension=1, tiled=True)  59.2 us
    all_gather x1, waiting for transfers between devices, body(): grad_all = lax.all_gather(grad_out, 'section', axis=0, tiled=True)  27.2 us
    all_gather x1, waiting for transfers between devices, body(): lax.all_gather(basis_act, ('dp', 'section'), axis=0, tiled=True)  23.1 us
    dot_general x1, matrix products, body(): jnp.dot(summed_rows, basis_cols, preferred_element_type=jnp.float32)  22.4 us
  transfers between devices with their start and end apart: 8, of which 6 were waited for; matrix products, arithmetic and copies ran while one was open for 11% of the time, Pallas kernels for 0%

commit v1 on v0

v1 whole, which is shorter than its diff:
```python
import jax
import jax.numpy as jnp
from jax import lax
from jax.sharding import PartitionSpec as P

damping = 0.1
bf16 = jnp.bfloat16
f32 = jnp.float32


def swap(x, axis, size, bit):
    return lax.ppermute(x, axis, [(i, i ^ bit) for i in range(size)])


def low_bit(m):
    return (m & -m).bit_length() - 1


def fetch(x, bits):
    got = [x]
    for m in range(1, 1 << len(bits)):
        low = low_bit(m)
        got.append(swap(got[m ^ (1 << low)], *bits[low]))
    return got


def fetch_split(x, bits):
    cut = x.shape[0] * 3 // 8 // 16 * 16
    got = [[x]]
    for m in range(1, 1 << len(bits)):
        low, high = low_bit(m), m.bit_length() - 1
        a, b = got[m ^ (1 << low)], got[m ^ (1 << high)]
        if low in (0, high):
            ways = [(piece, low) for piece in a]
        else:
            ways = [(jnp.concatenate(a, axis=0)[:cut], low), (jnp.concatenate(b, axis=0)[cut:], high)]
        pieces = []
        for piece, bit in ways:
            pieces.append(swap(piece, *bits[bit]))
        got.append(pieces)
    return got


def line_sum(part, size):
    total = part.astype(f32)
    last = None
    for h in range(1, size):
        send = part if last is None else (part.astype(f32) + last.astype(f32)).astype(bf16)
        last = lax.ppermute(send, "tensor", [(h - 1, h), (size - h, size - h - 1)])
        total = total + last.astype(f32)
    return total


def make_body(n_tensor, n_dp, n_section):
    def bits_of(axis, size):
        return [(axis, size, 1 << b) for b in range(size.bit_length() - 1)]

    section_bits = bits_of("section", n_section)
    plane_bits = section_bits + bits_of("dp", n_dp)
    n_plane = n_section * n_dp

    def body(basis_grad, query, basis_act, eig_vals, grad_out, act_in):
        return steps(basis_grad, query, basis_act, eig_vals, grad_out, act_in)

    def steps(basis_grad, query, basis_act, eig_vals, grad_out, act_in):
        t = lax.axis_index("tensor")
        s = lax.axis_index("section")
        r = lax.axis_index("dp") * n_section + s
        rows = basis_grad.shape[0]
        depth, cols = basis_act.shape
        share = cols // n_plane
        wide = act_in.shape[1]

        def all_tokens(x):
            got = fetch(x, section_bits)
            whole = jnp.zeros((x.shape[0] * n_section, x.shape[1]), x.dtype)
            for m, piece in enumerate(got):
                whole = lax.dynamic_update_slice(whole, piece, ((s ^ m) * x.shape[0], 0))
            return whole

        own = []
        for m in range(n_plane):
            part = lax.dynamic_slice_in_dim(basis_act, (r ^ m) * share, share, 1)
            if m:
                part = lax.ppermute(part, ("dp", "section"), [(i, i ^ m) for i in range(n_plane)])
            own.append(part)
        mine = jnp.concatenate(own, axis=0)
        basis = lax.all_gather(mine, "tensor", axis=1, tiled=True)
        act_tokens = all_tokens(act_in)
        grad_tokens = all_tokens(grad_out)
        queries = fetch_split(query, plane_bits)

        pieces = []
        for g in range(2):
            n = grad_tokens.shape[0] // 2
            part = jnp.einsum(
                "ti,ei->te", grad_tokens[g * n : (g + 1) * n], basis_grad, preferred_element_type=f32
            ).astype(bf16)
            pieces.append(line_sum(part, n_tensor).astype(bf16))
        grad_rot = jnp.concatenate(pieces, axis=0)

        act_part = 0.0
        for i in range(wide // depth):
            slot = (t * (wide // depth) + i) ^ r
            some = lax.dynamic_slice_in_dim(basis, slot * depth, depth, 0)
            act_part = act_part + jnp.dot(act_tokens[:, i * depth : (i + 1) * depth], some, preferred_element_type=f32)
        act_part = act_part.astype(bf16)
        basis, act_part = lax.optimization_barrier((basis, act_part))
        act_rot = lax.psum_scatter(act_part, "tensor", scatter_dimension=1, tiled=True)
        acts = fetch(act_rot, plane_bits)

        late = (n_plane - 2) * depth
        whole = [jnp.concatenate(pieces, axis=0) for pieces in queries[: n_plane - 2]]
        turned = jnp.dot(jnp.concatenate(whole, axis=1), basis[:late], preferred_element_type=f32)
        turns = []
        start = 0
        for pair in zip(*queries[n_plane - 2 :]):
            stop = start + pair[0].shape[0]
            term = jnp.dot(jnp.concatenate(pair, axis=1), basis[late:], preferred_element_type=f32)
            turns.append((turned[start:stop] + term).astype(bf16))
            start = stop
        turned = jnp.concatenate(turns, axis=0)
        turns = fetch(turned, plane_bits)

        precond = jnp.zeros((rows, cols), bf16)
        value = 0.0
        groups = [[0], [1]] + [[m, m + 1] for m in range(2, n_plane, 2)]
        for group in groups:
            parts = []
            for m in group:
                parts.append(jnp.dot(basis_grad, turns[m], preferred_element_type=f32).astype(bf16))
            rotated = lax.psum_scatter(
                jnp.concatenate(parts, axis=0), "tensor", scatter_dimension=1, tiled=True
            )
            for i, m in enumerate(group):
                place = (r ^ m) * share
                eig = lax.dynamic_slice_in_dim(eig_vals, place, share, 1)
                piece = (rotated[i * rows : (i + 1) * rows].astype(f32) / (eig + damping)).astype(bf16)
                precond = lax.dynamic_update_slice(precond, piece, (0, place))
                folded = jnp.dot(grad_rot, piece, preferred_element_type=f32)
                value = value + jnp.sum(folded * acts[m].astype(f32), axis=1)

        for axis, size, bit in plane_bits + bits_of("tensor", n_tensor):
            value = value + swap(value, axis, size, bit)
        out = value.shape[0] // n_tensor
        return (precond, lax.dynamic_slice_in_dim(value, t * out, out, 0))

    return body


def solution(mesh):
    sizes = tuple(mesh.shape[name] for name in ("tensor", "dp", "section"))
    return jax.shard_map(
        make_body(*sizes),
        mesh=mesh,
        in_specs=(
            P(("dp", "section"), "tensor"),
            P("tensor", ("dp", "section")),
            P(("dp", "section"), "tensor"),
            P(("dp", "section"), "tensor"),
            P("section", "tensor"),
            P("section", "tensor"),
        ),
        out_specs=(P(("dp", "section"), "tensor"), P("tensor")),
        check_vma=False,
    )
```

time: 957 us -> 719 us (0.75)
  waiting for transfers between devices: 818 us -> 374 us
  local copies, waits for them, and re-layouts: 0 us -> 79 us
  matrix products: 108 us -> 160 us
  starting transfers between devices: 0.5 us -> 51.2 us
  other arithmetic: 1.71 us -> 29.8 us
  blocking collectives: 13.7 us -> 0 us
    psum x1 -> x0, waiting for transfers between devices: 484 us -> none  [body(): summed_rows = lax.psum(partial_rows.astype(jnp.bfloat16), 'tensor')]
    ppermute x0 -> x47, waiting for transfers between devices: none -> 374 us  [the longest x34 290 us: swap(): return lax.ppermute(x, axis, [(i, i ^ bit) for i in range(size)])]
    all_gather x5 -> x1, waiting for transfers between devices: 202 us -> 0.01 us  [steps(): basis = lax.all_gather(mine, 'tensor', axis=1, tiled=True)]
    reduce_scatter x2 -> x5, waiting for transfers between devices: 130 us -> 0.03 us  [steps(): lax.psum_scatter(jnp.concatenate(parts, axis=0), 'tensor', scatter_dimens...]
    dot_general x5 -> x23, matrix products: 108 us -> 160 us  [the longest x8 99.7 us: steps(): jnp.dot(basis_grad, turns[m], preferred_element_type=f32).astype(bf16)]
    ppermute x0 -> x47, starting transfers between devices: none -> 50.1 us  [the longest x34 29.8 us: swap(): return lax.ppermute(x, axis, [(i, i ^ bit) for i in range(size)])]
    unnamed x0 -> x70, local copies, waits for them, and re-layouts: none -> 39.5 us
    convert_element_type x0 -> x11, other arithmetic: none -> 21.4 us  [the longest x5 8.39 us: steps(): (rotated[i * rows:(i + 1) * rows].astype(f32) / (eig + damping)).astype(b...]
  transfers between devices with their start and end apart: 8 -> 54, of which waited for: 6 -> 18; matrix products, arithmetic and copies ran while one was open for 11% -> 36% of each run, Pallas kernels for 0% -> 0%
where the time goes in v1:
time: 719 us; the launch traced here: 710 us
  waiting for transfers between devices  374 us (52%)
  matrix products  160 us (22%)
  local copies, waits for them, and re-layouts  79 us (11%)
  starting transfers between devices  51.2 us (7%)
  other arithmetic  29.8 us (4%)
  between operations  15.3 us (2%)
    ppermute x34, waiting for transfers between devices, swap(): return lax.ppermute(x, axis, [(i, i ^ bit) for i in range(size)])  290 us
    dot_general x8, matrix products, steps(): jnp.dot(basis_grad, turns[m], preferred_element_type=f32).astype(bf16)  99.7 us
    ppermute x6, waiting for transfers between devices, line_sum(): last = lax.ppermute(send, 'tensor', [(h - 1, h), (size - h, size - h - 1)])  78.6 us
    unnamed x70, local copies, waits for them, and re-layouts  39.5 us
    ppermute x34, starting transfers between devices, swap(): return lax.ppermute(x, axis, [(i, i ^ bit) for i in range(size)])  29.8 us
    dot_general x2, matrix products, steps(): jnp.einsum('ti,ei->te', grad_tokens[g * n:(g + 1) * n], basis_grad, prefe...  17.6 us
    dot_general x8, matrix products, steps(): folded = jnp.dot(grad_rot, piece, preferred_element_type=f32)  16.1 us
    dot_general x1, matrix products, steps(): jnp.dot(jnp.concatenate(whole, axis=1), basis[:late], preferred_element_t...  14.7 us
  transfers between devices with their start and end apart: 54, of which 18 were waited for; matrix products, arithmetic and copies ran while one was open for 36% of the time, Pallas kernels for 0%

profile of v1, /device:TPU:0, one launch (start us, length us, event | category | flops | bytes accessed | tf_op | source)
XLA Modules:
  0.0 709.7 jit_solution(14708583833498606570)
XLA Ops:
  19.9 5.4 collective-permute-done.9
  28.9 74.2 %collective-permute-done.1 = bf16[3584,512]{1,0:T(8,128)(2,1)} collective-permute-done((bf16[3584,512]{1,0:T(8,128)(2,1)}, bf16[3584,512]{1,0:T(8,128)(2,1)}, u32[]{:S(2)}, u32[]{:S(2)}) %collective-permute-start.1) | collective-permute-done | bytes 3670048 | tf_op jit(solution)/shard_map/ppermute | solution.py:12
  122.1 4.2 constant_dynamic-update-slice_fusion.4
  126.2 4.2 constant_dynamic-update-slice_fusion.3
  130.4 19.1 %collective-permute-done.15 = bf16[1344,512]{1,0:T(8,128)(2,1)} collective-permute-done((bf16[1344,512]{1,0:T(8,128)(2,1)S(1)}, bf16[1344,512]{1,0:T(8,128)(2,1)}, u32[]{:S(2)}, u32[]{:S(2)}) %collective-permute-start.15) | collective-permute-done | bytes 1376288 | tf_op jit(solution)/shard_map/ppermute | solution.py:12
  149.6 12.5 %collective-permute-done.17 = bf16[2240,512]{1,0:T(8,128)(2,1)} collective-permute-done((bf16[2240,512]{1,0:T(8,128)(2,1)S(1)}, bf16[2240,512]{1,0:T(8,128)(2,1)}, u32[]{:S(2)}, u32[]{:S(2)}) %collective-permute-start.17) | collective-permute-done | bytes 2293792 | tf_op jit(solution)/shard_map/ppermute | solution.py:12
  165.1 4.2 constant_dynamic-update-slice_fusion.2
  169.3 4.2 constant_dynamic-update-slice_fusion.1
  173.5 4.3 constant_dynamic-update-slice_fusion
  177.8 14.7 %fusion.7 = f32[3584,512]{1,0:T(8,128)S(1)} fusion(bf16[3584,3072]{1,0:T(8,128)(2,1)} %constant_dynamic-update-slice_fusion, bf16[4096,512]{1,0:T(8,128)(2,1)S(1)} %copy-done.23), kind=kOutput, calls=%fused_computation.10 | convolution fusion | flops 11274289152 | bytes 32505856 | tf_op jit(solution)/shard_map/dot_general | solution.py:114
  192.5 3.5 fusion.9
  196.0 5.6 fusion
  206.9 12.2 %fusion.16 = bf16[1792,512]{0,1:T(8,128)(2,1)} fusion(bf16[1792,3584]{1,0:T(8,128)(2,1)} %param.6, bf16[2240,512]{1,0:T(8,128)(2,1)S(1)} %fusion, bf16[1344,512]{1,0:T(8,128)(2,1)} %copy-done.14), kind=kOutput, calls=%fused_computation.26 | convolution fusion | flops 6584926208 | bytes 18350080 | tf_op jit(solution)/shard_map/dot_general | solution.py:131
  219.2 66.6 %collective-permute-done.20 = bf16[3584,512]{1,0:T(8,128)(2,1)} collective-permute-done((bf16[3584,512]{1,0:T(8,128)(2,1)}, bf16[3584,512]{1,0:T(8,128)(2,1)}, u32[]{:S(2)}, u32[]{:S(2)}) %collective-permute-start.20) | collective-permute-done | bytes 3670048 | tf_op jit(solution)/shard_map/ppermute | solution.py:12
  287.5 13.3 %fusion.17 = bf16[1792,512]{0,1:T(8,128)(2,1)} fusion(bf16[3584,512]{1,0:T(8,128)(2,1)} %collective-permute-done.19, bf16[1792,3584]{1,0:T(8,128)(2,1)} %param.6), kind=kOutput, calls=%fused_computation.27 | convolution fusion | flops 6577586176 | bytes 18350080 | tf_op jit(solution)/shard_map/dot_general | solution.py:131
  301.2 12.3 %fusion.18 = bf16[1792,512]{0,1:T(8,128)(2,1)S(1)} fusion(bf16[3584,512]{1,0:T(8,128)(2,1)} %collective-permute-done.20, bf16[1792,3584]{1,0:T(8,128)(2,1)} %param.6), kind=kOutput, calls=%fused_computation.28 | convolution fusion | flops 6577586176 | bytes 18350080 | tf_op jit(solution)/shard_map/dot_general | solution.py:131
  313.6 12.4 %fusion.19 = bf16[1792,512]{0,1:T(8,128)(2,1)S(1)} fusion(bf16[3584,512]{1,0:T(8,128)(2,1)} %collective-permute-done.21, bf16[1792,3584]{1,0:T(8,128)(2,1)} %param.6), kind=kOutput, calls=%fused_computation.29 | convolution fusion | flops 6577586176 | bytes 18350080 | tf_op jit(solution)/shard_map/dot_general | solution.py:131
  328.4 39.4 %collective-permute-done.22 = bf16[3584,512]{1,0:T(8,128)(2,1)} collective-permute-done((bf16[3584,512]{1,0:T(8,128)(2,1)}, bf16[3584,512]{1,0:T(8,128)(2,1)}, u32[]{:S(2)}, u32[]{:S(2)}) %collective-permute-start.22) | collective-permute-done | bytes 3670048 | tf_op jit(solution)/shard_map/ppermute | solution.py:12
  372.8 17.8 %collective-permute-done.27 = bf16[128,3584]{1,0:T(8,128)(2,1)S(1)} collective-permute-done((bf16[128,3584]{1,0:T(8,128)(2,1)S(1)}, bf16[128,3584]{1,0:T(8,128)(2,1)S(1)}, u32[]{:S(2)}, u32[]{:S(2)}) %collective-permute-start.27) | collective-permute-done | bytes 917536 | tf_op jit(solution)/shard_map/ppermute | solution.py:12
  393.3 12.4 %fusion.20 = bf16[1792,512]{0,1:T(8,128)(2,1)S(1)} fusion(bf16[3584,512]{1,0:T(8,128)(2,1)} %collective-permute-done.22, bf16[1792,3584]{1,0:T(8,128)(2,1)} %param.6), kind=kOutput, calls=%fused_computation.30 | convolution fusion | flops 6577586176 | bytes 18350080 | tf_op jit(solution)/shard_map/dot_general | solution.py:131
  405.7 12.4 %fusion.21 = bf16[1792,512]{0,1:T(8,128)(2,1)S(1)} fusion(bf16[3584,512]{1,0:T(8,128)(2,1)} %collective-permute-done.23, bf16[1792,3584]{1,0:T(8,128)(2,1)} %param.6), kind=kOutput, calls=%fused_computation.31 | convolution fusion | flops 6577586176 | bytes 18350080 | tf_op jit(solution)/shard_map/dot_general | solution.py:131
  422.2 51.4 %collective-permute-done.24 = bf16[3584,512]{1,0:T(8,128)(2,1)} collective-permute-done((bf16[3584,512]{1,0:T(8,128)(2,1)}, bf16[3584,512]{1,0:T(8,128)(2,1)}, u32[]{:S(2)}, u32[]{:S(2)}) %collective-permute-start.24) | collective-permute-done | bytes 3670048 | tf_op jit(solution)/shard_map/ppermute | solution.py:12
  473.7 8.8 %convolution_convert_fusion.9 = bf16[256,1792]{1,0:T(8,128)(2,1)S(1)} fusion(bf16[1792,3584]{1,0:T(8,128)(2,1)} %param.6, bf16[512,3584]{1,0:T(8,128)(2,1)} %constant_dynamic-update-slice_fusion.13), kind=kOutput, calls=%fused_computation.35 | convolution fusion | flops 3288793088 | bytes 15597568 | tf_op jit(solution)/shard_map/ti,ei->te/dot_general | solution.py:96
  482.5 3.9 collective-permute-start.29
  486.4 8.8 %convolution_convert_fusion.8 = bf16[256,1792]{1,0:T(8,128)(2,1)S(1)} fusion(bf16[1792,3584]{1,0:T(8,128)(2,1)} %param.6, bf16[512,3584]{1,0:T(8,128)(2,1)} %constant_dynamic-update-slice_fusion.13), kind=kOutput, calls=%fused_computation.34 | convolution fusion | flops 3288793088 | bytes 15597568 | tf_op jit(solution)/shard_map/ti,ei->te/dot_general | solution.py:96
  496.6 10.3 %collective-permute-done.29 = bf16[256,1792]{1,0:T(8,128)(2,1)S(1)} collective-permute-done((bf16[256,1792]{1,0:T(8,128)(2,1)S(1)}, bf16[256,1792]{1,0:T(8,128)(2,1)S(1)}, u32[]{:S(2)}, u32[]{:S(2)}) %collective-permute-start.29) | collective-permute-done | bytes 917536 | tf_op jit(solution)/shard_map/ppermute | solution.py:49
  510.6 12.3 %fusion.22 = bf16[1792,512]{0,1:T(8,128)(2,1)S(1)} fusion(bf16[3584,512]{1,0:T(8,128)(2,1)} %collective-permute-done.24, bf16[1792,3584]{1,0:T(8,128)(2,1)} %param.6), kind=kOutput, calls=%fused_computation.32 | convolution fusion | flops 6577586176 | bytes 18350080 | tf_op jit(solution)/shard_map/dot_general | solution.py:131
  523.0 12.3 %fusion.23 = bf16[1792,512]{0,1:T(8,128)(2,1)S(1)} fusion(bf16[3584,512]{1,0:T(8,128)(2,1)} %collective-permute-done.25, bf16[1792,3584]{1,0:T(8,128)(2,1)} %param.6), kind=kOutput, calls=%fused_computation.33 | convolution fusion | flops 6577586176 | bytes 18350080 | tf_op jit(solution)/shard_map/dot_general | solution.py:131
  547.8 6.0 constant_dynamic-slice_fusion
  572.6 45.9 %collective-permute-done.31 = bf16[256,1792]{1,0:T(8,128)(2,1)} collective-permute-done((bf16[256,1792]{1,0:T(8,128)(2,1)}, bf16[256,1792]{1,0:T(8,128)(2,1)}, u32[]{:S(2)}, u32[]{:S(2)}) %collective-permute-start.31) | collective-permute-done | bytes 917536 | tf_op jit(solution)/shard_map/ppermute | solution.py:49
  623.6 22.4 %collective-permute-done.34 = bf16[256,1792]{1,0:T(8,128)(2,1)} collective-permute-done((bf16[256,1792]{1,0:T(8,128)(2,1)}, bf16[256,1792]{1,0:T(8,128)(2,1)}, u32[]{:S(2)}, u32[]{:S(2)}) %collective-permute-start.34) | collective-permute-done | bytes 917536 | tf_op jit(solution)/shard_map/ppermute | solution.py:49
  692.3 3.4 collective-permute-start.45
  (232 shorter events, 154.1 us)
Async XLA Ops:
  7.2 155.0 %all-gather.2.cloned.1.call-start = ((), (), s32[]{:S(2)}) async-start(), calls=%async_computation.6 | async-start | bytes 5242880 | tf_op jit(solution)/shard_map/all_gather | solution.py:88
  18.5 84.6 %collective-permute-start.1 = (bf16[3584,512]{1,0:T(8,128)(2,1)}, bf16[3584,512]{1,0:T(8,128)(2,1)}, u32[]{:S(2)}, u32[]{:S(2)}) collective-permute-start(bf16[3584,512]{1,0:T(8,128)(2,1)} %param.7), channel_id=1, source_target_pairs={{0,2},{1,3},{2,0},{3,1},{4,6},{5,7},{6,4},{7,5},{8,10},{9,11},{10,... | collective-permute-start | bytes 11010056 | tf_op jit(solution)/shard_map/ppermute | solution.py:12
  26.4 544.7 %reduce-scatter.19.cloned.1.call-start = ((), (), s32[]{:S(2)}) async-start(), calls=%async_computation.12 | async-start | bytes 655360
  26.5 85.7 %collective-permute-start.3 = (bf16[3584,512]{1,0:T(8,128)(2,1)}, bf16[3584,512]{1,0:T(8,128)(2,1)}, u32[]{:S(2)}, u32[]{:S(2)}) collective-permute-start(bf16[3584,512]{1,0:T(8,128)(2,1)} %param.7), channel_id=1, source_target_pairs={{0,4},{4,0},{1,5},{5,1},{2,6},{6,2},{3,7},{7,3},{8,12},{12,8},{9,1... | collective-permute-start | bytes 11010056 | tf_op jit(solution)/shard_map/ppermute | solution.py:12
  28.4 93.7 %collective-permute-start = (bf16[3584,512]{1,0:T(8,128)(2,1)}, bf16[3584,512]{1,0:T(8,128)(2,1)}, u32[]{:S(2)}, u32[]{:S(2)}) collective-permute-start(bf16[3584,512]{1,0:T(8,128)(2,1)} %param.7), channel_id=1, source_target_pairs={{0,1},{1,0},{2,3},{3,2},{4,5},{5,4},{6,7},{7,6},{8,9},{9,8},{10,11... | collective-permute-start | bytes 11010056 | tf_op jit(solution)/shard_map/ppermute | solution.py:12
  103.1 62.0 %collective-permute-start.2 = (bf16[3584,512]{1,0:T(8,128)(2,1)}, bf16[3584,512]{1,0:T(8,128)(2,1)}, u32[]{:S(2)}, u32[]{:S(2)}) collective-permute-start(bf16[3584,512]{1,0:T(8,128)(2,1)} %collective-permute-done.1), channel_id=1, source_target_pairs={{0,1},{1,0},{2,3},{3,2},{4,5},{5,4},{6,7},{7,6},{8,9},{9,8},{10,11... | collective-permute-start | bytes 11010056 | tf_op jit(solution)/shard_map/ppermute | solution.py:12
  110.1 52.0 %collective-permute-start.17 = (bf16[2240,512]{1,0:T(8,128)(2,1)S(1)}, bf16[2240,512]{1,0:T(8,128)(2,1)}, u32[]{:S(2)}, u32[]{:S(2)}) collective-permute-start(bf16[2240,512]{1,0:T(8,128)(2,1)S(1)} %slice.70), channel_id=1, source_target_pairs={{0,4},{4,0},{1,5},{5,1},{2,6},{6,2},{3,7},{7,3},{8,12},{12,8},{9,1... | collective-permute-start | bytes 6881288 | tf_op jit(solution)/shard_map/ppermute | solution.py:12
  112.1 61.3 %collective-permute-start.4 = (bf16[3584,512]{1,0:T(8,128)(2,1)}, bf16[3584,512]{1,0:T(8,128)(2,1)}, u32[]{:S(2)}, u32[]{:S(2)}) collective-permute-start(bf16[3584,512]{1,0:T(8,128)(2,1)} %collective-permute-done.3), channel_id=1, source_target_pairs={{0,1},{1,0},{2,3},{3,2},{4,5},{5,4},{6,7},{7,6},{8,9},{9,8},{10,11... | collective-permute-start | bytes 11010056 | tf_op jit(solution)/shard_map/ppermute | solution.py:12
  117.3 32.3 %collective-permute-start.15 = (bf16[1344,512]{1,0:T(8,128)(2,1)S(1)}, bf16[1344,512]{1,0:T(8,128)(2,1)}, u32[]{:S(2)}, u32[]{:S(2)}) collective-permute-start(bf16[1344,512]{1,0:T(8,128)(2,1)S(1)} %slice.68), channel_id=1, source_target_pairs={{0,2},{1,3},{2,0},{3,1},{4,6},{5,7},{6,4},{7,5},{8,10},{9,11},{10,... | collective-permute-start | bytes 4128776 | tf_op jit(solution)/shard_map/ppermute | solution.py:12
  149.6 43.0 %collective-permute-start.16 = (bf16[1344,512]{1,0:T(8,128)(2,1)}, bf16[1344,512]{1,0:T(8,128)(2,1)}, u32[]{:S(2)}, u32[]{:S(2)}) collective-permute-start(bf16[1344,512]{1,0:T(8,128)(2,1)} %collective-permute-done.15), channel_id=1, source_target_pairs={{0,1},{1,0},{2,3},{3,2},{4,5},{5,4},{6,7},{7,6},{8,9},{9,8},{10,11... | collective-permute-start | bytes 4128776 | tf_op jit(solution)/shard_map/ppermute | solution.py:12
  162.1 33.9 %collective-permute-start.18 = (bf16[2240,512]{1,0:T(8,128)(2,1)}, bf16[2240,512]{1,0:T(8,128)(2,1)}, u32[]{:S(2)}, u32[]{:S(2)}) collective-permute-start(bf16[2240,512]{1,0:T(8,128)(2,1)} %collective-permute-done.17), channel_id=1, source_target_pairs={{0,1},{1,0},{2,3},{3,2},{4,5},{5,4},{6,7},{7,6},{8,9},{9,8},{10,11... | collective-permute-start | bytes 6881288 | tf_op jit(solution)/shard_map/ppermute | solution.py:12
  203.7 82.1 %collective-permute-start.20 = (bf16[3584,512]{1,0:T(8,128)(2,1)}, bf16[3584,512]{1,0:T(8,128)(2,1)}, u32[]{:S(2)}, u32[]{:S(2)}) collective-permute-start(bf16[3584,512]{1,0:T(8,128)(2,1)} %pad_maximum_fusion), channel_id=1, source_target_pairs={{0,2},{1,3},{2,0},{3,1},{4,6},{5,7},{6,4},{7,5},{8,10},{9,11},{10,... | collective-permute-start | bytes 11010056 | tf_op jit(solution)/shard_map/ppermute | solution.py:12
  205.4 82.1 %collective-permute-start.19 = (bf16[3584,512]{1,0:T(8,128)(2,1)}, bf16[3584,512]{1,0:T(8,128)(2,1)}, u32[]{:S(2)}, u32[]{:S(2)}) collective-permute-start(bf16[3584,512]{1,0:T(8,128)(2,1)} %pad_maximum_fusion), channel_id=1, source_target_pairs={{0,1},{1,0},{2,3},{3,2},{4,5},{5,4},{6,7},{7,6},{8,9},{9,8},{10,11... | collective-permute-start | bytes 11010056 | tf_op jit(solution)/shard_map/ppermute | solution.py:12
  206.7 443.3 %reduce-scatter.9.cloned.1.call-start = ((), (), s32[]{:S(2)}) async-start(), calls=%async_computation.7 | async-start | bytes 2293760 | tf_op jit(solution)/shard_map/reduce_scatter | solution.py:132
  219.1 437.5 %reduce-scatter.11.cloned.1.call-start = ((), (), s32[]{:S(2)}) async-start(), calls=%async_computation.8 | async-start | bytes 2293760 | tf_op jit(solution)/shard_map/reduce_scatter | solution.py:132
  285.8 27.8 %collective-permute-start.21 = (bf16[3584,512]{1,0:T(8,128)(2,1)}, bf16[3584,512]{1,0:T(8,128)(2,1)}, u32[]{:S(2)}, u32[]{:S(2)}) collective-permute-start(bf16[3584,512]{1,0:T(8,128)(2,1)} %collective-permute-done.20), channel_id=1, source_target_pairs={{0,1},{1,0},{2,3},{3,2},{4,5},{5,4},{6,7},{7,6},{8,9},{9,8},{10,11... | collective-permute-start | bytes 11010056 | tf_op jit(solution)/shard_map/ppermute | solution.py:12
  285.8 82.1 %collective-permute-start.22 = (bf16[3584,512]{1,0:T(8,128)(2,1)}, bf16[3584,512]{1,0:T(8,128)(2,1)}, u32[]{:S(2)}, u32[]{:S(2)}) collective-permute-start(bf16[3584,512]{1,0:T(8,128)(2,1)} %pad_maximum_fusion), channel_id=1, source_target_pairs={{0,4},{4,0},{1,5},{5,1},{2,6},{6,2},{3,7},{7,3},{8,12},{12,8},{9,1... | collective-permute-start | bytes 11010056 | tf_op jit(solution)/shard_map/ppermute | solution.py:12
  300.8 361.5 %reduce-scatter.13.cloned.1.call-start = ((), (), s32[]{:S(2)}) async-start(), calls=%async_computation.9 | async-start | bytes 4587520 | tf_op jit(solution)/shard_map/reduce_scatter | solution.py:132
  328.2 344.0 %reduce-scatter.15.cloned.1.call-start = ((), (), s32[]{:S(2)}) async-start(), calls=%async_computation.10 | async-start | bytes 4587520 | tf_op jit(solution)/shard_map/reduce_scatter | solution.py:132
  367.8 37.9 %collective-permute-start.23 = (bf16[3584,512]{1,0:T(8,128)(2,1)}, bf16[3584,512]{1,0:T(8,128)(2,1)}, u32[]{:S(2)}, u32[]{:S(2)}) collective-permute-start(bf16[3584,512]{1,0:T(8,128)(2,1)} %collective-permute-done.22), channel_id=1, source_target_pairs={{0,1},{1,0},{2,3},{3,2},{4,5},{5,4},{6,7},{7,6},{8,9},{9,8},{10,11... | collective-permute-start | bytes 11010056 | tf_op jit(solution)/shard_map/ppermute | solution.py:12
  390.6 30.7 %collective-permute-start.28 = (bf16[128,3584]{1,0:T(8,128)(2,1)S(1)}, bf16[128,3584]{1,0:T(8,128)(2,1)S(1)}, u32[]{:S(2)}, u32[]{:S(2)}) collective-permute-start(bf16[128,3584]{1,0:T(8,128)(2,1)S(1)} %collective-permute-done.27), channel_id=1, source_target_pairs={{0,1},{1,0},{2,3},{3,2},{4,5},{5,4},{6,7},{7,6},{8,9},{9,8},{10,11... | collective-permute-start | bytes 2752520 | tf_op jit(solution)/shard_map/ppermute | solution.py:12
  391.6 82.1 %collective-permute-start.24 = (bf16[3584,512]{1,0:T(8,128)(2,1)}, bf16[3584,512]{1,0:T(8,128)(2,1)}, u32[]{:S(2)}, u32[]{:S(2)}) collective-permute-start(bf16[3584,512]{1,0:T(8,128)(2,1)} %collective-permute-done.22), channel_id=1, source_target_pairs={{0,2},{1,3},{2,0},{3,1},{4,6},{5,7},{6,4},{7,5},{8,10},{9,11},{10,... | collective-permute-start | bytes 11010056 | tf_op jit(solution)/shard_map/ppermute | solution.py:12
  420.2 258.0 %reduce-scatter.17.cloned.1.call-start = ((), (), s32[]{:S(2)}) async-start(), calls=%async_computation.11 | async-start | bytes 4587520 | tf_op jit(solution)/shard_map/reduce_scatter | solution.py:132
  473.7 49.3 %collective-permute-start.25 = (bf16[3584,512]{1,0:T(8,128)(2,1)}, bf16[3584,512]{1,0:T(8,128)(2,1)}, u32[]{:S(2)}, u32[]{:S(2)}) collective-permute-start(bf16[3584,512]{1,0:T(8,128)(2,1)} %collective-permute-done.24), channel_id=1, source_target_pairs={{0,1},{1,0},{2,3},{3,2},{4,5},{5,4},{6,7},{7,6},{8,9},{9,8},{10,11... | collective-permute-start | bytes 11010056 | tf_op jit(solution)/shard_map/ppermute | solution.py:12
  495.2 42.2 %collective-permute-start.32 = (bf16[256,1792]{1,0:T(8,128)(2,1)S(1)}, bf16[256,1792]{1,0:T(8,128)(2,1)S(1)}, u32[]{:S(2)}, u32[]{:S(2)}) collective-permute-start(bf16[256,1792]{1,0:T(8,128)(2,1)S(1)} %convolution_convert_fusion.8), channel_id=1, source_target_pairs={{0,8},{24,16},{1,9},{25,17},{2,10},{26,18},{3,11},{27,19},{4,12},{... | collective-permute-start | bytes 2752520 | tf_op jit(solution)/shard_map/ppermute | solution.py:49
  509.0 31.2 %collective-permute-start.30 = (bf16[256,1792]{1,0:T(8,128)(2,1)}, bf16[256,1792]{1,0:T(8,128)(2,1)}, u32[]{:S(2)}, u32[]{:S(2)}) collective-permute-start(bf16[256,1792]{1,0:T(8,128)(2,1)} %fusion.32), channel_id=1, source_target_pairs={{8,16},{16,8},{9,17},{17,9},{10,18},{18,10},{11,19},{19,11},{12,20... | collective-permute-start | bytes 2752520 | tf_op jit(solution)/shard_map/ppermute | solution.py:49
  542.6 75.9 %collective-permute-start.31 = (bf16[256,1792]{1,0:T(8,128)(2,1)}, bf16[256,1792]{1,0:T(8,128)(2,1)}, u32[]{:S(2)}, u32[]{:S(2)}) collective-permute-start(bf16[256,1792]{1,0:T(8,128)(2,1)} %fusion.26), channel_id=1, source_target_pairs={{16,24},{8,0},{17,25},{9,1},{18,26},{10,2},{19,27},{11,3},{20,28},... | collective-permute-start | bytes 2752520 | tf_op jit(solution)/shard_map/ppermute | solution.py:49
  546.2 99.8 %collective-permute-start.34 = (bf16[256,1792]{1,0:T(8,128)(2,1)}, bf16[256,1792]{1,0:T(8,128)(2,1)}, u32[]{:S(2)}, u32[]{:S(2)}) collective-permute-start(bf16[256,1792]{1,0:T(8,128)(2,1)} %fusion.29), channel_id=1, source_target_pairs={{16,24},{8,0},{17,25},{9,1},{18,26},{10,2},{19,27},{11,3},{20,28},... | collective-permute-start | bytes 2752520 | tf_op jit(solution)/shard_map/ppermute | solution.py:49
  571.1 52.0 %collective-permute-start.38 = (bf16[512,128]{0,1:T(8,128)(2,1)}, bf16[512,128]{0,1:T(8,128)(2,1)}, u32[]{:S(2)}, u32[]{:S(2)}) collective-permute-start(bf16[512,128]{0,1:T(8,128)(2,1)} %bitcast.46), channel_id=1, source_target_pairs={{0,4},{4,0},{1,5},{5,1},{2,6},{6,2},{3,7},{7,3},{8,12},{12,8},{9,1... | collective-permute-start | bytes 393224 | tf_op jit(solution)/shard_map/ppermute | solution.py:12
  621.6 27.8 %collective-permute-start.36 = (bf16[512,128]{0,1:T(8,128)(2,1)S(1)}, bf16[512,128]{0,1:T(8,128)(2,1)}, u32[]{:S(2)}, u32[]{:S(2)}) collective-permute-start(bf16[512,128]{0,1:T(8,128)(2,1)S(1)} %bitcast.47), channel_id=1, source_target_pairs={{0,2},{1,3},{2,0},{3,1},{4,6},{5,7},{6,4},{7,5},{8,10},{9,11},{10,... | collective-permute-start | bytes 393224 | tf_op jit(solution)/shard_map/ppermute | solution.py:12
  648.9 26.8 %collective-permute-start.39 = (bf16[512,128]{0,1:T(8,128)(2,1)}, bf16[512,128]{0,1:T(8,128)(2,1)}, u32[]{:S(2)}, u32[]{:S(2)}) collective-permute-start(bf16[512,128]{0,1:T(8,128)(2,1)} %collective-permute-done.38), channel_id=1, source_target_pairs={{0,1},{1,0},{2,3},{3,2},{4,5},{5,4},{6,7},{7,6},{8,9},{9,8},{10,11... | collective-permute-start | bytes 393224 | tf_op jit(solution)/shard_map/ppermute | solution.py:12
  649.4 34.4 %collective-permute-start.41 = (bf16[512,128]{0,1:T(8,128)(2,1)}, bf16[512,128]{0,1:T(8,128)(2,1)S(1)}, u32[]{:S(2)}, u32[]{:S(2)}) collective-permute-start(bf16[512,128]{0,1:T(8,128)(2,1)} %collective-permute-done.40), channel_id=1, source_target_pairs={{0,1},{1,0},{2,3},{3,2},{4,5},{5,4},{6,7},{7,6},{8,9},{9,8},{10,11... | collective-permute-start | bytes 393224 | tf_op jit(solution)/shard_map/ppermute | solution.py:12
  (47 other events, 584.5 us)
Sparse Core Ops, SparseCore 0:
  26.5 82.6 all-gather.1
  206.8 22.1 reduce-scatter.18
  231.3 37.7 reduce-scatter.8
  300.9 39.7 reduce-scatter.10
  342.9 67.5 reduce-scatter.12
  420.3 68.8 reduce-scatter.14
  537.6 98.3 reduce-scatter.16

commit v2 on v1

v2 whole, which is shorter than its diff:
```python
import functools
import math

import jax
import jax.numpy as jnp
from jax import lax
from jax.experimental import pallas as pl
from jax.sharding import PartitionSpec as P

damping = 0.1
bf16 = jnp.bfloat16
f32 = jnp.float32
plane = ("dp", "section")


def swap(x, axis, size, bit):
    return lax.ppermute(x, axis, [(i, i ^ bit) for i in range(size)])


def low_bit(m):
    return (m & -m).bit_length() - 1


def fetch(x, bits):
    got = [x]
    for m in range(1, 1 << len(bits)):
        low = low_bit(m)
        got.append(swap(got[m ^ (1 << low)], *bits[low]))
    return got


def fetch_split(x, bits, cut):
    got = [[x]]
    for m in range(1, 1 << len(bits)):
        low, high = low_bit(m), m.bit_length() - 1
        a, b = got[m ^ (1 << low)], got[m ^ (1 << high)]
        if m == 2:
            ways = [(x[:cut], low), (x[cut:], low)]
        elif low in (0, high):
            ways = [(piece, low) for piece in a]
        else:
            ways = [(a[0] if len(a) > 1 else a[0][:cut], low), (b[1] if len(b) > 1 else b[0][cut:], high)]
        pieces = []
        for piece, bit in ways:
            pieces.append(swap(piece, *bits[bit]))
        got.append(pieces)
    return got


def line_sum(part, size):
    total = part.astype(f32)
    last = None
    for h in range(1, size):
        send = part if last is None else (part.astype(f32) + last.astype(f32)).astype(bf16)
        last = lax.ppermute(send, "tensor", [(h - 1, h), (size - h, size - h - 1)])
        total = total + last.astype(f32)
    return total


def cost(flops, arrays):
    size = sum(math.prod(x.shape) * x.dtype.itemsize for x in arrays)
    return pl.CostEstimate(flops=flops, bytes_accessed=size, transcendentals=0)


def turn_kernel(depth, cut, counts, *refs):
    refs = list(refs)
    out, basis = refs.pop(), refs.pop()
    blocks = [[refs.pop() for _ in range(count)][::-1] for count in reversed(counts)][::-1]
    at = pl.program_id(0)

    def run(side):
        value = refs[0][...] if refs else None
        for m, pieces in enumerate(blocks):
            term = jnp.dot(
                pieces[min(side, len(pieces) - 1)][...],
                basis[m * depth : (m + 1) * depth],
                preferred_element_type=f32,
            )
            value = term if value is None else value + term
        out[...] = value.astype(out.dtype)

    @pl.when(at < cut)
    def _():
        run(0)

    @pl.when(at >= cut)
    def _():
        run(1)


def turn(total, blocks, basis, cut, dtype):
    rows = sum(piece.shape[0] for piece in blocks[0])
    depth = blocks[0][0].shape[1]
    cols = basis.shape[1]
    step = math.gcd(cut, rows)
    n = cut // step
    part = depth * len(blocks)
    place = 0 if total is None else basis.shape[0] // part - 1
    whole = pl.BlockSpec((step, depth), lambda i: (i, 0))
    first = pl.BlockSpec((step, depth), lambda i: (jnp.minimum(i, n - 1), 0))
    second = pl.BlockSpec((step, depth), lambda i: (jnp.maximum(i - n, 0), 0))
    tile = pl.BlockSpec((step, cols), lambda i: (i, 0))
    specs = [] if total is None else [tile]
    flat = [] if total is None else [total]
    for pieces in blocks:
        specs += [whole] if len(pieces) == 1 else [first, second]
        flat += pieces
    out = jax.ShapeDtypeStruct((rows, cols), dtype)
    return pl.pallas_call(
        functools.partial(turn_kernel, depth, n, [len(pieces) for pieces in blocks]),
        grid=(rows // step,),
        in_specs=specs + [pl.BlockSpec((part, cols), lambda i: (place, 0))],
        out_specs=tile,
        out_shape=out,
        cost_estimate=cost(2 * rows * part * cols, [*flat, out]),
    )(*flat, basis)


def pair_kernel(left, *refs):
    *rights, out = refs
    share = out.shape[-1]
    for i, right in enumerate(rights):
        value = jnp.dot(left[...], right[...], preferred_element_type=f32).astype(out.dtype)
        for z in range(out.shape[0]):
            out[z, i] = value[:, z * share : (z + 1) * share]


def pair_dot(left, rights, groups, step):
    rows, depth = left.shape
    cols = rights[0].shape[1]
    out = jax.ShapeDtypeStruct((groups, len(rights), rows, cols // groups), bf16)
    return pl.pallas_call(
        pair_kernel,
        grid=(rows // step,),
        in_specs=[pl.BlockSpec((step, depth), lambda i: (i, 0))]
        + [pl.BlockSpec((depth, cols), lambda i: (0, 0))] * len(rights),
        out_specs=pl.BlockSpec((groups, len(rights), step, cols // groups), lambda i: (0, 0, i, 0)),
        out_shape=out,
        cost_estimate=cost(2 * rows * depth * cols * len(rights), [left, *rights, out]),
    )(left, *rights)


def make_body(n_tensor, n_dp, n_section):
    def bits_of(axis, size):
        return [(axis, size, 1 << b) for b in range(size.bit_length() - 1)]

    section_bits = bits_of("section", n_section)
    plane_bits = section_bits + bits_of("dp", n_dp)
    n_plane = n_section * n_dp
    n_early = n_plane - 2

    def steps(basis_grad, query, basis_act, eig_vals, grad_out, act_in):
        t = lax.axis_index("tensor")
        s = lax.axis_index("section")
        r = lax.axis_index("dp") * n_section + s
        rows, units = basis_grad.shape
        depth, cols = basis_act.shape
        share = cols // n_plane
        wide = act_in.shape[1]
        cut = units * 3 // 8 // 16 * 16

        def all_tokens(x):
            got = fetch(x, section_bits)
            whole = jnp.zeros((x.shape[0] * n_section, x.shape[1]), x.dtype)
            for m, piece in enumerate(got):
                whole = lax.dynamic_update_slice(whole, piece, ((s ^ m) * x.shape[0], 0))
            return whole

        own = []
        for m in range(n_plane):
            part = lax.dynamic_slice_in_dim(basis_act, (r ^ m) * share, share, 1)
            if m:
                part = lax.ppermute(part, plane, [(i, i ^ m) for i in range(n_plane)])
            own.append(part)
        mine = jnp.concatenate(own, axis=0)
        basis = lax.all_gather(mine, "tensor", axis=1, tiled=True)
        act_tokens = all_tokens(act_in)
        grad_tokens = all_tokens(grad_out)
        queries = fetch_split(query, plane_bits, cut)

        pieces = []
        for g in range(2):
            n = grad_tokens.shape[0] // 2
            part = jnp.einsum(
                "ti,ei->te", grad_tokens[g * n : (g + 1) * n], basis_grad, preferred_element_type=f32
            ).astype(bf16)
            pieces.append(line_sum(part, n_tensor).astype(bf16))
        grad_rot = jnp.concatenate(pieces, axis=0)

        act_part = 0.0
        for i in range(wide // depth):
            slot = (t * (wide // depth) + i) ^ r
            some = lax.dynamic_slice_in_dim(basis, slot * depth, depth, 0)
            act_part = act_part + jnp.dot(
                act_tokens[:, i * depth : (i + 1) * depth], some, preferred_element_type=f32
            )
        act_rot = lax.psum_scatter(act_part.astype(bf16), "tensor", scatter_dimension=1, tiled=True)
        acts = fetch(act_rot, plane_bits)

        turned = turn(None, queries[:n_early], basis, cut, f32)
        turned = turn(turned, queries[n_early:], basis, cut, bf16)
        turns = fetch(turned, plane_bits)

        precond = jnp.zeros((rows, cols), bf16)
        value = 0.0
        for m in range(0, n_plane, 2):
            parts = pair_dot(basis_grad, turns[m : m + 2], n_tensor, math.gcd(rows, 256))
            parts = parts.reshape(n_tensor, 2 * rows, share)
            rotated = lax.psum_scatter(parts, "tensor", scatter_dimension=0, tiled=False)
            for i in range(2):
                place = (r ^ (m + i)) * share
                eig = lax.dynamic_slice_in_dim(eig_vals, place, share, 1)
                piece = (rotated[i * rows : (i + 1) * rows].astype(f32) / (eig + damping)).astype(bf16)
                precond = lax.dynamic_update_slice(precond, piece, (0, place))
                folded = jnp.dot(grad_rot, piece, preferred_element_type=f32)
                value = value + jnp.sum(folded * acts[m + i].astype(f32), axis=1)

        for axis, size, bit in plane_bits + bits_of("tensor", n_tensor):
            value = value + swap(value, axis, size, bit)
        out = value.shape[0] // n_tensor
        return (precond, lax.dynamic_slice_in_dim(value, t * out, out, 0))

    return steps


def solution(mesh):
    sizes = tuple(mesh.shape[name] for name in ("tensor", "dp", "section"))
    weight = P(plane, "tensor")
    tokens = P("section", "tensor")
    return jax.shard_map(
        make_body(*sizes),
        mesh=mesh,
        in_specs=(weight, P("tensor", plane), weight, weight, tokens, tokens),
        out_specs=(weight, P("tensor")),
        check_vma=False,
    )
```

time: 719 us -> 768 us (1.068); the launches traced: 710 us -> 767 us
  waiting for transfers between devices: 374 us -> 535 us
  matrix products: 160 us -> 23.3 us
  Pallas kernels: 0 us -> 106 us
  local copies, waits for them, and re-layouts: 79 us -> 12.4 us
    dot_general x11 -> x0, matrix products: 123 us -> none  [the longest x8 99.7 us: steps(): jnp.dot(basis_grad, turns[m], preferred_element_type=f32).astype(bf16)]
    pallas_call x0 -> x6, Pallas kernels: none -> 106 us  [the longest x4 76.2 us: pair_dot(): pl.pallas_call(pair_kernel, grid=(rows // step,), in_specs=[pl.BlockSpec(...]
    ppermute x7, waiting for transfers between devices: 6.08 us -> 81.8 us  [steps(): part = lax.ppermute(part, plane, [(i, i ^ m) for i in range(n_plane)])]
    ppermute x34 -> x36, waiting for transfers between devices: 290 us -> 332 us  [swap(): return lax.ppermute(x, axis, [(i, i ^ bit) for i in range(size)])]
    ppermute x6, waiting for transfers between devices: 78.6 us -> 121 us  [line_sum(): last = lax.ppermute(send, 'tensor', [(h - 1, h), (size - h, size - h - 1)])]
    unnamed x70 -> x34, local copies, waits for them, and re-layouts: 39.5 us -> 3.9 us
    dynamic_update_slice x0 -> x8, other arithmetic: none -> 17.7 us  [steps(): precond = lax.dynamic_update_slice(precond, piece, (0, place))]
    dot_general x8, matrix products: 16.1 us -> 6.05 us  [steps(): folded = jnp.dot(grad_rot, piece, preferred_element_type=f32)]
  transfers between devices with their start and end apart: 54 -> 55, of which waited for: 18 -> 26; matrix products, arithmetic and copies ran while one was open for 36% -> 8% of each run, Pallas kernels for 0% -> 12%
where the time goes in v2:
time: 768 us; the launch traced here: 767 us
  waiting for transfers between devices  535 us (70%)
  Pallas kernels  106 us (14%)
  starting transfers between devices  45.2 us (6%)
  other arithmetic  29.8 us (4%)
  matrix products  23.3 us (3%)
  between operations  14.6 us (2%)
  local copies, waits for them, and re-layouts  12.4 us (2%)
    ppermute x36, waiting for transfers between devices, swap(): return lax.ppermute(x, axis, [(i, i ^ bit) for i in range(size)])  332 us
    ppermute x6, waiting for transfers between devices, line_sum(): last = lax.ppermute(send, 'tensor', [(h - 1, h), (size - h, size - h - 1)])  121 us
    ppermute x7, waiting for transfers between devices, steps(): part = lax.ppermute(part, plane, [(i, i ^ m) for i in range(n_plane)])  81.8 us
    pallas_call x4, Pallas kernels, pair_dot(): pl.pallas_call(pair_kernel, grid=(rows // step,), in_specs=[pl.BlockSpec(...  76.2 us
    pallas_call x2, Pallas kernels, turn(): pl.pallas_call(functools.partial(turn_kernel, depth, n, [len(pieces) for...  30.3 us
    ppermute x36, starting transfers between devices, swap(): return lax.ppermute(x, axis, [(i, i ^ bit) for i in range(size)])  26.8 us
    dynamic_update_slice x8, other arithmetic, steps(): precond = lax.dynamic_update_slice(precond, piece, (0, place))  17.7 us
  transfers between devices with their start and end apart: 55, of which 26 were waited for; matrix products, arithmetic and copies ran while one was open for 8% of the time, Pallas kernels for 12%

profile of v2, /device:TPU:0, one launch (start us, length us, event | category | flops | bytes accessed | tf_op | source)
XLA Modules:
  0.0 766.8 jit_solution(2988814650278685563)
XLA Ops:
  7.2 3.1 collective-permute-start.5
  15.3 2.9 collective-permute-done.8
  21.7 77.4 %collective-permute-done.10 = bf16[512,128]{1,0:T(8,128)(2,1)S(1)} collective-permute-done((bf16[512,128]{1,0:T(8,128)(2,1)S(1)}, bf16[512,128]{1,0:T(8,128)(2,1)S(1)}, u32[]{:S(2)}, u32[]{:S(2)}) %collective-permute-start.10) | collective-permute-done | bytes 131104 | tf_op jit(solution)/shard_map/ppermute | solution.py:173
  106.4 49.9 %collective-permute-done.2.refs_3_ = bf16[2240,512]{1,0:T(8,128)(2,1)S(1)} collective-permute-done((bf16[2240,512]{1,0:T(8,128)(2,1)S(1)}, bf16[2240,512]{1,0:T(8,128)(2,1)S(1)}, u32[]{:S(2)}, u32[]{:S(2)}) %collective-permute-start.2) | collective-permute-done | bytes 2293792 | tf_op jit(solution)/shard_map/ppermute | solution.py:17
  157.6 27.7 %collective-permute-done.1.refs_2_ = bf16[1344,512]{1,0:T(8,128)(2,1)S(1)} collective-permute-done((bf16[1344,512]{1,0:T(8,128)(2,1)S(1)}, bf16[1344,512]{1,0:T(8,128)(2,1)S(1)}, u32[]{:S(2)}, u32[]{:S(2)}) %collective-permute-start.1) | collective-permute-done | bytes 1376288 | tf_op jit(solution)/shard_map/ppermute | solution.py:17
  190.2 17.6 %collective-permute-done.15.refs_2_ = bf16[2240,512]{1,0:T(8,128)(2,1)S(1)} collective-permute-done((bf16[2240,512]{1,0:T(8,128)(2,1)S(1)}, bf16[2240,512]{1,0:T(8,128)(2,1)S(1)}, u32[]{:S(2)}, u32[]{:S(2)}) %collective-permute-start.15) | collective-permute-done | bytes 2293792 | tf_op jit(solution)/shard_map/ppermute | solution.py:17
  207.8 13.0 %collective-permute-done.14.refs_1_ = bf16[1344,512]{1,0:T(8,128)(2,1)} collective-permute-done((bf16[1344,512]{1,0:T(8,128)(2,1)S(1)}, bf16[1344,512]{1,0:T(8,128)(2,1)}, u32[]{:S(2)}, u32[]{:S(2)}) %collective-permute-start.14) | collective-permute-done | bytes 1376288 | tf_op jit(solution)/shard_map/ppermute | solution.py:17
  222.7 18.6 %shard_map.77.refs_0_ = f32[3584,512]{1,0:T(8,128)} custom-call(bf16[3584,512]{1,0:T(8,128)(2,1)} %refs_0_.1, bf16[3584,512]{1,0:T(8,128)(2,1)} %copy-done.9, bf16[1344,512]{1,0:T(8,128)(2,1)} %copy-done.11, bf16[2240,512]{1,0:T(8,128)(2,1)} %copy-done.10, bf16[1344,512]{1,0:T(8,128)(2,1)} %copy-done.12, bf16[2240,512]{1,0:T(8,128)(2,1)} %collective-permute-done.4.refs_5_, ...), custom_call_target="tpu_custom_call" | custom-call | flops 11274289152 | bytes 29360128 | tf_op jit(solution)/shard_map/pallas_call | solution.py:109
  241.3 11.7 %shard_map.78.refs_0_ = bf16[3584,512]{1,0:T(8,128)(2,1)} custom-call(f32[3584,512]{1,0:T(8,128)} %shard_map.77.refs_0_, bf16[1344,512]{1,0:T(8,128)(2,1)} %collective-permute-done.14.refs_1_, bf16[2240,512]{1,0:T(8,128)(2,1)} %copy-done.2, bf16[1344,512]{1,0:T(8,128)(2,1)} %collective-permute-done.16.refs_3_, ...), custom_call_target="tpu_custom_call" | custom-call | flops 3758096384 | bytes 18350080 | tf_op jit(solution)/shard_map/pallas_call | solution.py:109
  255.2 6.6 collective-permute-done.35
  264.8 2.4 fusion.10
  269.0 19.0 %shard_map.79 = bf16[4,2,1792,128]{3,2,1,0:T(8,128)(2,1)} custom-call(bf16[1792,3584]{1,0:T(8,128)(2,1)} %left.7, bf16[3584,512]{1,0:T(8,128)(2,1)} %shard_map.78.refs_0_, bf16[3584,512]{1,0:T(8,128)(2,1)} %collective-permute-done.18.refs_1_), custom_call_target="tpu_custom_call" | custom-call | flops 13153337344 | bytes 23855104 | tf_op jit(solution)/shard_map/pallas_call | solution.py:132
  288.1 60.9 %collective-permute-done.19.refs_0_ = bf16[3584,512]{1,0:T(8,128)(2,1)} collective-permute-done((bf16[3584,512]{1,0:T(8,128)(2,1)}, bf16[3584,512]{1,0:T(8,128)(2,1)}, u32[]{:S(2)}, u32[]{:S(2)}) %collective-permute-start.19) | collective-permute-done | bytes 3670048 | tf_op jit(solution)/shard_map/ppermute | solution.py:17
  350.8 5.0 collective-permute-done.20.refs_1_
  355.8 19.0 %shard_map.80 = bf16[4,2,1792,128]{3,2,1,0:T(8,128)(2,1)} custom-call(bf16[1792,3584]{1,0:T(8,128)(2,1)} %left.7, bf16[3584,512]{1,0:T(8,128)(2,1)} %collective-permute-done.19.refs_0_, bf16[3584,512]{1,0:T(8,128)(2,1)} %collective-permute-done.20.refs_1_), custom_call_target="tpu_custom_call" | custom-call | flops 13153337344 | bytes 23855104 | tf_op jit(solution)/shard_map/pallas_call | solution.py:132
  374.9 56.2 %collective-permute-done.21.refs_0_ = bf16[3584,512]{1,0:T(8,128)(2,1)} collective-permute-done((bf16[3584,512]{1,0:T(8,128)(2,1)}, bf16[3584,512]{1,0:T(8,128)(2,1)}, u32[]{:S(2)}, u32[]{:S(2)}) %collective-permute-start.21) | collective-permute-done | bytes 3670048 | tf_op jit(solution)/shard_map/ppermute | solution.py:17
  432.8 5.0 collective-permute-done.22.refs_1_
  437.8 19.1 %shard_map.81 = bf16[4,2,1792,128]{3,2,1,0:T(8,128)(2,1)} custom-call(bf16[1792,3584]{1,0:T(8,128)(2,1)} %left.7, bf16[3584,512]{1,0:T(8,128)(2,1)} %collective-permute-done.21.refs_0_, bf16[3584,512]{1,0:T(8,128)(2,1)} %collective-permute-done.22.refs_1_), custom_call_target="tpu_custom_call" | custom-call | flops 13153337344 | bytes 23855104 | tf_op jit(solution)/shard_map/pallas_call | solution.py:132
  460.2 72.5 %collective-permute-done.26 = bf16[128,3584]{1,0:T(8,128)(2,1)S(1)} collective-permute-done((bf16[128,3584]{1,0:T(8,128)(2,1)S(1)}, bf16[128,3584]{1,0:T(8,128)(2,1)S(1)}, u32[]{:S(2)}, u32[]{:S(2)}) %collective-permute-start.26) | collective-permute-done | bytes 917536 | tf_op jit(solution)/shard_map/ppermute | solution.py:17
  535.3 6.7 convolution_convert_fusion.1
  541.9 3.8 collective-permute-start.28
  545.7 6.7 convolution_convert_fusion
  553.7 12.6 %collective-permute-done.28 = bf16[256,1792]{1,0:T(8,128)(2,1)S(1)} collective-permute-done((bf16[256,1792]{1,0:T(8,128)(2,1)S(1)}, bf16[256,1792]{1,0:T(8,128)(2,1)S(1)}, u32[]{:S(2)}, u32[]{:S(2)}) %collective-permute-start.28) | collective-permute-done | bytes 917536 | tf_op jit(solution)/shard_map/ppermute | solution.py:55
  569.2 16.0 %collective-permute-done.31 = bf16[256,1792]{1,0:T(8,128)(2,1)S(1)} collective-permute-done((bf16[256,1792]{1,0:T(8,128)(2,1)S(1)}, bf16[256,1792]{1,0:T(8,128)(2,1)S(1)}, u32[]{:S(2)}, u32[]{:S(2)}) %collective-permute-start.31) | collective-permute-done | bytes 917536 | tf_op jit(solution)/shard_map/ppermute | solution.py:55
  588.0 19.0 %shard_map.82 = bf16[4,2,1792,128]{3,2,1,0:T(8,128)(2,1)} custom-call(bf16[1792,3584]{1,0:T(8,128)(2,1)} %left.7, bf16[3584,512]{1,0:T(8,128)(2,1)} %collective-permute-done.23.refs_0_, bf16[3584,512]{1,0:T(8,128)(2,1)} %collective-permute-done.24.refs_1_), custom_call_target="tpu_custom_call" | custom-call | flops 13153337344 | bytes 23855104 | tf_op jit(solution)/shard_map/pallas_call | solution.py:132
  607.1 2.3 fusion.2
  616.2 66.6 %collective-permute-done.30 = bf16[256,1792]{1,0:T(8,128)(2,1)} collective-permute-done((bf16[256,1792]{1,0:T(8,128)(2,1)}, bf16[256,1792]{1,0:T(8,128)(2,1)}, u32[]{:S(2)}, u32[]{:S(2)}) %collective-permute-start.30) | collective-permute-done | bytes 917536 | tf_op jit(solution)/shard_map/ppermute | solution.py:55
  682.8 3.1 fusion.1
  687.9 25.7 %collective-permute-done.33 = bf16[256,1792]{1,0:T(8,128)(2,1)} collective-permute-done((bf16[256,1792]{1,0:T(8,128)(2,1)}, bf16[256,1792]{1,0:T(8,128)(2,1)}, u32[]{:S(2)}, u32[]{:S(2)}) %collective-permute-start.33) | collective-permute-done | bytes 917536 | tf_op jit(solution)/shard_map/ppermute | solution.py:55
  724.8 2.3 constant_dynamic-update-slice_fusion.20
  751.3 3.6 collective-permute-done.47
  754.9 4.5 collective-permute-done.48
  (175 shorter events, 91.8 us)
Async XLA Ops:
  7.2 215.5 %all-gather.2.cloned.1.call-start = ((), (), s32[]{:S(2)}) async-start(), calls=%async_computation.5 | async-start | bytes 5242880 | tf_op jit(solution)/shard_map/all_gather | solution.py:176
  7.2 99.1 %collective-permute-start.5 = (bf16[3584,512]{1,0:T(8,128)(2,1)}, bf16[3584,512]{1,0:T(8,128)(2,1)}, u32[]{:S(2)}, u32[]{:S(2)}) collective-permute-start(bf16[3584,512]{1,0:T(8,128)(2,1)} %refs_0_.1), channel_id=1, source_target_pairs={{0,4},{4,0},{1,5},{5,1},{2,6},{6,2},{3,7},{7,3},{8,12},{12,8},{9,1... | collective-permute-start | bytes 11010056 | tf_op jit(solution)/shard_map/ppermute | solution.py:17
  13.6 85.5 %collective-permute-start.10 = (bf16[512,128]{1,0:T(8,128)(2,1)S(1)}, bf16[512,128]{1,0:T(8,128)(2,1)S(1)}, u32[]{:S(2)}, u32[]{:S(2)}) collective-permute-start(bf16[512,128]{1,0:T(8,128)(2,1)S(1)} %get-tuple-element.20), channel_id=1, source_target_pairs={{0,4},{1,5},{2,6},{3,7},{4,0},{5,1},{6,2},{7,3},{8,12},{9,13},{10,... | collective-permute-start | bytes 393224 | tf_op jit(solution)/shard_map/ppermute | solution.py:173
  13.8 86.5 %collective-permute-start.11 = (bf16[512,128]{1,0:T(8,128)(2,1)S(1)}, bf16[512,128]{1,0:T(8,128)(2,1)S(1)}, u32[]{:S(2)}, u32[]{:S(2)}) collective-permute-start(bf16[512,128]{1,0:T(8,128)(2,1)S(1)} %get-tuple-element.19), channel_id=1, source_target_pairs={{0,5},{1,4},{2,7},{3,6},{4,1},{5,0},{6,3},{7,2},{8,13},{9,12},{10,... | collective-permute-start | bytes 393224 | tf_op jit(solution)/shard_map/ppermute | solution.py:173
  18.2 82.2 %collective-permute-start.12 = (bf16[512,128]{1,0:T(8,128)(2,1)S(1)}, bf16[512,128]{1,0:T(8,128)(2,1)S(1)}, u32[]{:S(2)}, u32[]{:S(2)}) collective-permute-start(bf16[512,128]{1,0:T(8,128)(2,1)S(1)} %get-tuple-element.25), channel_id=1, source_target_pairs={{0,6},{1,7},{2,4},{3,5},{4,2},{5,3},{6,0},{7,1},{8,14},{9,15},{10,... | collective-permute-start | bytes 393224 | tf_op jit(solution)/shard_map/ppermute | solution.py:173
  20.0 80.4 %collective-permute-start.13 = (bf16[512,128]{1,0:T(8,128)(2,1)S(1)}, bf16[512,128]{1,0:T(8,128)(2,1)S(1)}, u32[]{:S(2)}, u32[]{:S(2)}) collective-permute-start(bf16[512,128]{1,0:T(8,128)(2,1)S(1)} %get-tuple-element.18), channel_id=1, source_target_pairs={{0,7},{1,6},{2,5},{3,4},{4,3},{5,2},{6,1},{7,0},{8,15},{9,14},{10,... | collective-permute-start | bytes 393224 | tf_op jit(solution)/shard_map/ppermute | solution.py:173
  101.4 513.1 %reduce-scatter.14.cloned.1.call-start = ((), (), s32[]{:S(2)}) async-start(), calls=%async_computation.10 | async-start | bytes 655360 | tf_op jit(solution)/shard_map/reduce_scatter | solution.py:197
  103.4 52.8 %collective-permute-start.2 = (bf16[2240,512]{1,0:T(8,128)(2,1)S(1)}, bf16[2240,512]{1,0:T(8,128)(2,1)S(1)}, u32[]{:S(2)}, u32[]{:S(2)}) collective-permute-start(bf16[2240,512]{1,0:T(8,128)(2,1)S(1)} %slice.54), channel_id=1, source_target_pairs={{0,2},{1,3},{2,0},{3,1},{4,6},{5,7},{6,4},{7,5},{8,10},{9,11},{10,... | collective-permute-start | bytes 6881288 | tf_op jit(solution)/shard_map/ppermute | solution.py:17
  105.1 80.2 %collective-permute-start.1 = (bf16[1344,512]{1,0:T(8,128)(2,1)S(1)}, bf16[1344,512]{1,0:T(8,128)(2,1)S(1)}, u32[]{:S(2)}, u32[]{:S(2)}) collective-permute-start(bf16[1344,512]{1,0:T(8,128)(2,1)S(1)} %slice.53), channel_id=1, source_target_pairs={{0,2},{1,3},{2,0},{3,1},{4,6},{5,7},{6,4},{7,5},{8,10},{9,11},{10,... | collective-permute-start | bytes 4128776 | tf_op jit(solution)/shard_map/ppermute | solution.py:17
  105.9 114.9 %collective-permute-start = (bf16[3584,512]{1,0:T(8,128)(2,1)S(1)}, bf16[3584,512]{1,0:T(8,128)(2,1)S(1)}, u32[]{:S(2)}, u32[]{:S(2)}) collective-permute-start(bf16[3584,512]{1,0:T(8,128)(2,1)S(1)} %copy-done), channel_id=1, source_target_pairs={{0,1},{1,0},{2,3},{3,2},{4,5},{5,4},{6,7},{7,6},{8,9},{9,8},{10,11... | collective-permute-start | bytes 11010056 | tf_op jit(solution)/shard_map/ppermute | solution.py:17
  106.4 116.3 %collective-permute-start.6 = (bf16[3584,512]{1,0:T(8,128)(2,1)}, bf16[3584,512]{1,0:T(8,128)(2,1)}, u32[]{:S(2)}, u32[]{:S(2)}) collective-permute-start(bf16[3584,512]{1,0:T(8,128)(2,1)} %collective-permute-done.5.refs_6_), channel_id=1, source_target_pairs={{0,1},{1,0},{2,3},{3,2},{4,5},{5,4},{6,7},{7,6},{8,9},{9,8},{10,11... | collective-permute-start | bytes 11010056 | tf_op jit(solution)/shard_map/ppermute | solution.py:17
  156.2 51.5 %collective-permute-start.15 = (bf16[2240,512]{1,0:T(8,128)(2,1)S(1)}, bf16[2240,512]{1,0:T(8,128)(2,1)S(1)}, u32[]{:S(2)}, u32[]{:S(2)}) collective-permute-start(bf16[2240,512]{1,0:T(8,128)(2,1)S(1)} %collective-permute-done.2.refs_3_), channel_id=1, source_target_pairs={{0,4},{4,0},{1,5},{5,1},{2,6},{6,2},{3,7},{7,3},{8,12},{12,8},{9,1... | collective-permute-start | bytes 6881288 | tf_op jit(solution)/shard_map/ppermute | solution.py:17
  185.3 37.3 %collective-permute-start.4 = (bf16[2240,512]{1,0:T(8,128)(2,1)S(1)}, bf16[2240,512]{1,0:T(8,128)(2,1)}, u32[]{:S(2)}, u32[]{:S(2)}) collective-permute-start(bf16[2240,512]{1,0:T(8,128)(2,1)S(1)} %collective-permute-done.2.refs_3_), channel_id=1, source_target_pairs={{0,1},{1,0},{2,3},{3,2},{4,5},{5,4},{6,7},{7,6},{8,9},{9,8},{10,11... | collective-permute-start | bytes 6881288 | tf_op jit(solution)/shard_map/ppermute | solution.py:17
  188.4 32.3 %collective-permute-start.14 = (bf16[1344,512]{1,0:T(8,128)(2,1)S(1)}, bf16[1344,512]{1,0:T(8,128)(2,1)}, u32[]{:S(2)}, u32[]{:S(2)}) collective-permute-start(bf16[1344,512]{1,0:T(8,128)(2,1)S(1)} %slice.68), channel_id=1, source_target_pairs={{0,2},{1,3},{2,0},{3,1},{4,6},{5,7},{6,4},{7,5},{8,10},{9,11},{10,... | collective-permute-start | bytes 4128776 | tf_op jit(solution)/shard_map/ppermute | solution.py:17
  207.8 33.5 %collective-permute-start.17 = (bf16[2240,512]{1,0:T(8,128)(2,1)S(1)}, bf16[2240,512]{1,0:T(8,128)(2,1)}, u32[]{:S(2)}, u32[]{:S(2)}) collective-permute-start(bf16[2240,512]{1,0:T(8,128)(2,1)S(1)} %collective-permute-done.15.refs_2_), channel_id=1, source_target_pairs={{0,1},{1,0},{2,3},{3,2},{4,5},{5,4},{6,7},{7,6},{8,9},{9,8},{10,11... | collective-permute-start | bytes 6881288 | tf_op jit(solution)/shard_map/ppermute | solution.py:17
  267.2 449.4 %reduce-scatter.6.cloned.1.call-start = ((), (), s32[]{:S(2)}) async-start(), calls=%async_computation.6 | async-start | bytes 4587520 | tf_op jit(solution)/shard_map/reduce_scatter | solution.py:209
  267.3 81.8 %collective-permute-start.19 = (bf16[3584,512]{1,0:T(8,128)(2,1)}, bf16[3584,512]{1,0:T(8,128)(2,1)}, u32[]{:S(2)}, u32[]{:S(2)}) collective-permute-start(bf16[3584,512]{1,0:T(8,128)(2,1)} %shard_map.78.refs_0_), channel_id=1, source_target_pairs={{0,2},{1,3},{2,0},{3,1},{4,6},{5,7},{6,4},{7,5},{8,10},{9,11},{10,... | collective-permute-start | bytes 11010056 | tf_op jit(solution)/shard_map/ppermute | solution.py:17
  288.1 436.6 %reduce-scatter.8.cloned.1.call-start = ((), (), s32[]{:S(2)}) async-start(), calls=%async_computation.7 | async-start | bytes 4587520 | tf_op jit(solution)/shard_map/reduce_scatter | solution.py:209
  349.0 82.1 %collective-permute-start.21 = (bf16[3584,512]{1,0:T(8,128)(2,1)}, bf16[3584,512]{1,0:T(8,128)(2,1)}, u32[]{:S(2)}, u32[]{:S(2)}) collective-permute-start(bf16[3584,512]{1,0:T(8,128)(2,1)} %shard_map.78.refs_0_), channel_id=1, source_target_pairs={{0,4},{4,0},{1,5},{5,1},{2,6},{6,2},{3,7},{7,3},{8,12},{12,8},{9,1... | collective-permute-start | bytes 11010056 | tf_op jit(solution)/shard_map/ppermute | solution.py:17
  374.8 355.2 %reduce-scatter.10.cloned.1.call-start = ((), (), s32[]{:S(2)}) async-start(), calls=%async_computation.8 | async-start | bytes 4587520 | tf_op jit(solution)/shard_map/reduce_scatter | solution.py:209
  431.1 101.8 %collective-permute-start.23 = (bf16[3584,512]{1,0:T(8,128)(2,1)}, bf16[3584,512]{1,0:T(8,128)(2,1)}, u32[]{:S(2)}, u32[]{:S(2)}) collective-permute-start(bf16[3584,512]{1,0:T(8,128)(2,1)} %collective-permute-done.21.refs_0_), channel_id=1, source_target_pairs={{0,2},{1,3},{2,0},{3,1},{4,6},{5,7},{6,4},{7,5},{8,10},{9,11},{10,... | collective-permute-start | bytes 11010056 | tf_op jit(solution)/shard_map/ppermute | solution.py:17
  457.0 279.9 %reduce-scatter.12.cloned.1.call-start = ((), (), s32[]{:S(2)}) async-start(), calls=%async_computation.9 | async-start | bytes 4587520 | tf_op jit(solution)/shard_map/reduce_scatter | solution.py:209
  458.1 74.6 %collective-permute-start.26 = (bf16[128,3584]{1,0:T(8,128)(2,1)S(1)}, bf16[128,3584]{1,0:T(8,128)(2,1)S(1)}, u32[]{:S(2)}, u32[]{:S(2)}) collective-permute-start(bf16[128,3584]{1,0:T(8,128)(2,1)S(1)} %copy-done.6), channel_id=1, source_target_pairs={{0,2},{1,3},{2,0},{3,1},{4,6},{5,7},{6,4},{7,5},{8,10},{9,11},{10,... | collective-permute-start | bytes 2752520 | tf_op jit(solution)/shard_map/ppermute | solution.py:17
  459.8 72.9 %collective-permute-start.25 = (bf16[128,3584]{1,0:T(8,128)(2,1)S(1)}, bf16[128,3584]{1,0:T(8,128)(2,1)S(1)}, u32[]{:S(2)}, u32[]{:S(2)}) collective-permute-start(bf16[128,3584]{1,0:T(8,128)(2,1)S(1)} %copy-done.6), channel_id=1, source_target_pairs={{0,1},{1,0},{2,3},{3,2},{4,5},{5,4},{6,7},{7,6},{8,9},{9,8},{10,11... | collective-permute-start | bytes 2752520 | tf_op jit(solution)/shard_map/ppermute | solution.py:17
  532.9 55.1 %collective-permute-start.24 = (bf16[3584,512]{1,0:T(8,128)(2,1)}, bf16[3584,512]{1,0:T(8,128)(2,1)}, u32[]{:S(2)}, u32[]{:S(2)}) collective-permute-start(bf16[3584,512]{1,0:T(8,128)(2,1)} %collective-permute-done.23.refs_0_), channel_id=1, source_target_pairs={{0,1},{1,0},{2,3},{3,2},{4,5},{5,4},{6,7},{7,6},{8,9},{9,8},{10,11... | collective-permute-start | bytes 11010056 | tf_op jit(solution)/shard_map/ppermute | solution.py:17
  552.4 32.8 %collective-permute-start.31 = (bf16[256,1792]{1,0:T(8,128)(2,1)S(1)}, bf16[256,1792]{1,0:T(8,128)(2,1)S(1)}, u32[]{:S(2)}, u32[]{:S(2)}) collective-permute-start(bf16[256,1792]{1,0:T(8,128)(2,1)S(1)} %convolution_convert_fusion), channel_id=1, source_target_pairs={{0,8},{24,16},{1,9},{25,17},{2,10},{26,18},{3,11},{27,19},{4,12},{... | collective-permute-start | bytes 2752520 | tf_op jit(solution)/shard_map/ppermute | solution.py:55
  567.6 39.5 %collective-permute-start.29 = (bf16[256,1792]{1,0:T(8,128)(2,1)}, bf16[256,1792]{1,0:T(8,128)(2,1)}, u32[]{:S(2)}, u32[]{:S(2)}) collective-permute-start(bf16[256,1792]{1,0:T(8,128)(2,1)} %fusion.8), channel_id=1, source_target_pairs={{8,16},{16,8},{9,17},{17,9},{10,18},{18,10},{11,19},{19,11},{12,20... | collective-permute-start | bytes 2752520 | tf_op jit(solution)/shard_map/ppermute | solution.py:55
  609.4 73.3 %collective-permute-start.30 = (bf16[256,1792]{1,0:T(8,128)(2,1)}, bf16[256,1792]{1,0:T(8,128)(2,1)}, u32[]{:S(2)}, u32[]{:S(2)}) collective-permute-start(bf16[256,1792]{1,0:T(8,128)(2,1)} %fusion.2), channel_id=1, source_target_pairs={{16,24},{8,0},{17,25},{9,1},{18,26},{10,2},{19,27},{11,3},{20,28},... | collective-permute-start | bytes 2752520 | tf_op jit(solution)/shard_map/ppermute | solution.py:55
  613.0 100.6 %collective-permute-start.33 = (bf16[256,1792]{1,0:T(8,128)(2,1)}, bf16[256,1792]{1,0:T(8,128)(2,1)}, u32[]{:S(2)}, u32[]{:S(2)}) collective-permute-start(bf16[256,1792]{1,0:T(8,128)(2,1)} %fusion.5), channel_id=1, source_target_pairs={{16,24},{8,0},{17,25},{9,1},{18,26},{10,2},{19,27},{11,3},{20,28},... | collective-permute-start | bytes 2752520 | tf_op jit(solution)/shard_map/ppermute | solution.py:55
  614.6 72.8 %collective-permute-start.40 = (bf16[512,128]{0,1:T(8,128)(2,1)}, bf16[512,128]{0,1:T(8,128)(2,1)S(1)}, u32[]{:S(2)}, u32[]{:S(2)}) collective-permute-start(bf16[512,128]{0,1:T(8,128)(2,1)} %reduce-scatter.14.cloned.1.call-done), channel_id=1, source_target_pairs={{0,4},{4,0},{1,5},{5,1},{2,6},{6,2},{3,7},{7,3},{8,12},{12,8},{9,1... | collective-permute-start | bytes 393224 | tf_op jit(solution)/shard_map/ppermute | solution.py:17
  685.9 30.2 %collective-permute-start.38 = (bf16[512,128]{0,1:T(8,128)(2,1)S(1)}, bf16[512,128]{0,1:T(8,128)(2,1)S(1)}, u32[]{:S(2)}, u32[]{:S(2)}) collective-permute-start(bf16[512,128]{0,1:T(8,128)(2,1)S(1)} %copy-done.13), channel_id=1, source_target_pairs={{0,2},{1,3},{2,0},{3,1},{4,6},{5,7},{6,4},{7,5},{8,10},{9,11},{10,... | collective-permute-start | bytes 393224 | tf_op jit(solution)/shard_map/ppermute | solution.py:17
  687.4 28.8 %collective-permute-start.42 = (bf16[512,128]{0,1:T(8,128)(2,1)S(1)}, bf16[512,128]{0,1:T(8,128)(2,1)S(1)}, u32[]{:S(2)}, u32[]{:S(2)}) collective-permute-start(bf16[512,128]{0,1:T(8,128)(2,1)S(1)} %collective-permute-done.40), channel_id=1, source_target_pairs={{0,2},{1,3},{2,0},{3,1},{4,6},{5,7},{6,4},{7,5},{8,10},{9,11},{10,... | collective-permute-start | bytes 393224 | tf_op jit(solution)/shard_map/ppermute | solution.py:17
  (37 other events, 516.5 us)
Sparse Core Ops, SparseCore 0:
  101.5 82.2 all-gather.1
  267.3 23.2 reduce-scatter.13
  293.0 66.9 reduce-scatter.5
  375.0 70.0 reduce-scatter.7
  457.1 70.0 reduce-scatter.9
  607.2 99.8 reduce-scatter.11
